TPU v7x, 256 devices: a whole 4x4x8 slice. The times are simulated.
256 devices in a mesh: seq: 64 (over z_lo, y, x, core), chan: 4 (over z_hi).
Axes of the slice: x: 4, y: 4, z: 8 (z_hi: 4, z_lo: 2; z = z_hi * 2 + z_lo), core: 2. Of those that a mesh axis runs over, the one named last changes fastest.
Arguments:
- features: bfloat16 [3, 2, 8192, 8192], P(None, None, 'chan', 'seq'), may hold values from -6 to 6
- offsets: int32 [2], replicated, may hold values from 0 to 4095
- tokens: int32 [2, 4], replicated, may hold values from 0 to 511
- decay_rate: float32 [16, 8192], P(None, 'chan'), may hold values from 0 to 1
- residue: float32 [16, 8192], P(None, 'chan'), may hold values from -1 to 1
- skip_weight: float32 [8192], P('chan'), may hold values from -3 to 3
- embedding: bfloat16 [512, 8192], P(None, 'seq'), may hold values from -12 to 12
- norm_gain: float32 [8192], P('seq'), may hold values from 0.1 to 1.9
- dec_weight: bfloat16 [3, 8192, 8192], P(None, 'seq', 'chan'), may hold values from -0.1875 to 0.1875
- out_weight: bfloat16 [8192, 8192], P('chan', 'seq'), may hold values from -0.1875 to 0.1875
Outputs:
- mixed: bfloat16 [2, 8192, 8192], P(None, 'chan', 'seq')
- decoded: bfloat16 [2, 4, 8192], P(None, None, ('seq', 'chan'))
All inputs are finite; a program needn't handle non-finite values.
Results may differ from a plain program's by a relative error of at most 0.0082.
Values may be sent and summed in bfloat16 or wider, within the bound.
No kernel may reach another device: no remote copies, remote signals or barrier semaphores. Data moves between devices by JAX's collectives and lax.ppermute only.
A program may use at most 128 MiB of HBM per device.

v0:
```python
import math
import jax
import jax.numpy as jnp
from jax import lax
from jax.sharding import PartitionSpec as P

D = 8192
highest = lax.Precision.HIGHEST


def local_conv(signal, rates, residues, skips, start_state):
    batch_rows, channels, length = signal.shape
    modes = rates.shape[0]
    block = math.gcd(length, 256)
    blocks = length // block
    group = math.gcd(channels, max(1, 2**21 // (block * block)))
    groups = channels // group

    def one_group(packed):
        sig_group, rate_group, res_group, skip_group, start_group = packed
        expo = -rate_group
        lag_pos = jnp.arange(block, dtype=jnp.float32)
        filt = jnp.sum(res_group[:, :, None] * jnp.exp(expo[:, :, None] * lag_pos), axis=0)
        distance = jnp.arange(block)[:, None] - jnp.arange(block)[None, :]
        toeplitz = jnp.where(distance >= 0, jnp.take(filt, jnp.maximum(distance, 0), axis=1), 0.0)
        blocked = sig_group.reshape(batch_rows, group, blocks, block)
        inner = jnp.einsum("gij,bgnj->bgni", toeplitz, blocked, precision=highest)
        tail_weight = jnp.exp(expo[:, :, None] * (block - 1.0 - lag_pos))
        block_sums = jnp.einsum("mgj,bgnj->bmgn", tail_weight, blocked, precision=highest)
        block_pos = jnp.arange(blocks, dtype=jnp.float32)
        block_gap = block_pos[:, None] - 1.0 - block_pos[None, :]
        spread = jnp.where(
            block_gap >= 0,
            jnp.exp(expo[:, :, None, None] * block * jnp.maximum(block_gap, 0.0)),
            0.0,
        )
        carried = jnp.einsum("mgnk,bmgk->bmgn", spread, block_sums, precision=highest)
        carried = (
            carried + jnp.exp(expo[:, :, None] * block * block_pos)[None] * start_group[..., None]
        )
        head_weight = res_group[:, :, None] * jnp.exp(expo[:, :, None] * (lag_pos + 1.0))
        outer = jnp.einsum("mgi,bmgn->bgni", head_weight, carried, precision=highest)
        conv = (inner + outer).reshape(batch_rows, group, length) + skip_group[
            None, :, None
        ] * sig_group
        final = jnp.exp(expo * block)[None] * carried[..., -1] + block_sums[..., -1]
        return (conv, final)

    packed = (
        signal.reshape(batch_rows, groups, group, length).transpose(1, 0, 2, 3),
        rates.reshape(modes, groups, group).transpose(1, 0, 2),
        residues.reshape(modes, groups, group).transpose(1, 0, 2),
        skips.reshape(groups, group),
        start_state.reshape(batch_rows, modes, groups, group).transpose(2, 0, 1, 3),
    )
    conv, final = lax.map(one_group, packed)
    conv = conv.transpose(1, 0, 2, 3).reshape(batch_rows, channels, length)
    final = final.transpose(1, 2, 0, 3).reshape(batch_rows, modes, channels)
    return (conv, final)


def body(
    features,
    offsets,
    tokens,
    decay_rate,
    residue,
    skip_weight,
    embedding,
    norm_gain,
    dec_weight,
    out_weight,
):
    seq_count = lax.axis_size("seq")
    seq_index = lax.axis_index("seq")
    query = features[0]
    keys_in = features[1]
    values_in = features[2]
    batch_rows, local_chans, shard_len = query.shape
    modes = decay_rate.shape[0]
    positions = seq_index * shard_len + jnp.arange(shard_len, dtype=jnp.int32)
    live = positions[None, :] >= offsets[:, None]
    product = jnp.where(
        live[:, None, :], keys_in.astype(jnp.float32) * values_in.astype(jnp.float32), 0.0
    ).astype(jnp.bfloat16)
    per_device = local_chans // seq_count
    own_rates = lax.dynamic_slice_in_dim(decay_rate, seq_index * per_device, per_device, 1)
    own_residue = lax.dynamic_slice_in_dim(residue, seq_index * per_device, per_device, 1)
    own_skip = lax.dynamic_slice_in_dim(skip_weight, seq_index * per_device, per_device, 0)
    query_part = lax.all_to_all(query, "seq", split_axis=1, concat_axis=2, tiled=True)
    signal_part = lax.all_to_all(product, "seq", split_axis=1, concat_axis=2, tiled=True)
    item_rows = query_part.shape[0]
    start = jnp.zeros((item_rows, modes, per_device), jnp.float32)
    conv, final = local_conv(
        signal_part.astype(jnp.float32), own_rates, own_residue, own_skip, start
    )
    gated = (query_part.astype(jnp.float32) * conv).astype(jnp.bfloat16)
    returned = lax.all_to_all(gated, "seq", split_axis=2, concat_axis=1, tiled=True)
    steps = tokens.shape[1]
    vocab = embedding.shape[0]
    flat_tokens = tokens.reshape(-1)
    one_hot = (flat_tokens[:, None] == jnp.arange(vocab, dtype=jnp.int32)[None, :]).astype(
        jnp.bfloat16
    )
    embedded = jnp.dot(one_hot, embedding, preferred_element_type=jnp.float32)
    partial_sq = jnp.sum(embedded * embedded, axis=1)
    total_sq = lax.psum(partial_sq, "seq")
    normed = (embedded * lax.rsqrt(total_sq / D + 1e-05)[:, None] * norm_gain[None, :]).astype(
        jnp.bfloat16
    )
    proj_terms = jnp.einsum("td,idc->itc", normed, dec_weight, preferred_element_type=jnp.float32)
    projected = lax.psum_scatter(proj_terms, "seq", scatter_dimension=2, tiled=True).astype(
        jnp.bfloat16
    )
    projected = projected.reshape(3, batch_rows, steps, per_device)
    decay = jnp.exp(-own_rates)
    running = final
    outputs = []
    for step in range(steps):
        rounded = lax.optimization_barrier(
            (
                projected[1, :, step].astype(jnp.float32)
                * projected[2, :, step].astype(jnp.float32)
            ).astype(jnp.bfloat16)
        )
        mixed_in = rounded.astype(jnp.float32)
        running = decay[None] * running + mixed_in[:, None, :]
        conv_step = jnp.sum(own_residue[None] * running, axis=1) + own_skip[None] * mixed_in
        outputs.append((projected[0, :, step].astype(jnp.float32) * conv_step).astype(jnp.bfloat16))
    decode_mix = jnp.stack(outputs, axis=1)
    piece = lax.all_gather(decode_mix, "seq", axis=2, tiled=True)
    piece_width = piece.shape[2]
    summed = jnp.dot(piece.reshape(-1, piece_width), out_weight, preferred_element_type=jnp.float32)
    decoded = lax.psum_scatter(summed, "chan", scatter_dimension=1, tiled=True).astype(jnp.bfloat16)
    decoded = decoded.reshape(batch_rows, steps, -1)
    return (returned, decoded)


def solution(mesh):
    placed = (
        P(None, None, "chan", "seq"),
        P(),
        P(),
        P(None, "chan"),
        P(None, "chan"),
        P("chan"),
        P(None, "seq"),
        P("seq"),
        P(None, "seq", "chan"),
        P("chan", "seq"),
    )
    return jax.shard_map(
        body,
        mesh=mesh,
        in_specs=placed,
        out_specs=(P(None, "chan", "seq"), P(None, None, ("seq", "chan"))),
        check_vma=False,
    )
```

profile of v0, /device:TPU:2, one launch (start us, length us, event | category | flops | bytes accessed | tf_op | source)
XLA Modules:
  0.0 975.1 jit_solution(962015850110151932)
XLA Ops:
  7.2 0.0 copy-start
  7.2 0.0 copy-start.5
  7.2 3.5 fusion.69
  10.8 0.7 broadcast_compare_fusion
  11.5 13.2 %fusion.19 = bf16[2,2048,128]{2,0,1:T(2,128)(2,1)} fusion(pred[2,128]{1,0:T(4,128)(4,1)S(1)} %broadcast_compare_fusion, bf16[1,2,2048,128]{3,2,1,0:T(8,128)(2,1)} %get-tuple-element.31, bf16[1,2,2048,128]{3,2,1,0:T(8,128)(2,1)S(1)} %get-tuple-element.30), kind=kLoop, calls=%fused_computation.24 | loop fusion | flops 2621440 | bytes 3145984 | tf_op jit(solution)/shard_map/convert_element_type | solution.py:85
  24.7 9.4 all-to-all-start.1
  34.0 0.8 fusion.68
  34.8 0.1 copy.127
  34.9 0.1 fusion.43
  35.0 0.1 fusion.44
  35.1 0.1 eq.15
  35.2 0.1 copy.126
  35.3 0.3 multiply_reduce_fusion.5
  35.6 0.3 multiply_reduce_fusion
  35.9 0.1 copy.174
  36.0 3.6 copy.213
  39.6 0.1 exponential_multiply_fusion
  39.8 10.8 %all-to-all-done.1 = bf16[2,2048,128]{2,0,1:T(2,128)(2,1)S(1)} async-done(((bf16[2,2048,128]{2,0,1:T(2,128)(2,1)}), bf16[2,2048,128]{2,0,1:T(2,128)(2,1)S(1)}, u32[]{:S(2)}, u32[]{:S(2)}) %all-to-all-start.1) | async-done | bytes 1048608 | tf_op jit(solution)/shard_map/all_to_all | solution.py:91
  50.6 5.7 all-to-all-start
  56.4 141.6 %psum.7 = f32[8]{0:T(128)S(1)} all-reduce(f32[8]{0:T(128)S(1)} %get-tuple-element.52), channel_id=1, replica_groups=mesh['seq'=64,'chan'=4] {'seq'}, use_global_device_ids=true, to_apply=%region_2.3 | all-reduce | flops 8 | bytes 64 | tf_op jit(solution)/shard_map/psum | solution.py:107
  198.0 0.8 dynamic_slice.25
  198.8 0.1 copy.128
  198.9 217.0 %gather_fusion = f32[65536,32]{1,0:T(8,128)} fusion(f32[32,256]{0,1:T(8,128)S(1)} %copy.128, s32[65536]{0:T(1024)S(1)} %broadcast_clamp_fusion), kind=kCustom, calls=%fused_computation | custom fusion | bytes 17039360 | tf_op jit(solution)/shard_map/while/body/eval_jaxpr/jit(_take)/gather | solution.py:25
  415.9 22.2 %copy.129 = f32[256,256,32]{1,0,2:T(8,128)} copy(f32[256,256,32]{2,1,0:T(8,128)} %bitcast.138) | data formatting | bytes 16777216 | tf_op jit(solution)/shard_map/while/body/eval_jaxpr/jit(_take)/gather | solution.py:25
  438.1 0.1 maximum_compare_fusion
  438.2 2.9 copy_bitcast_fusion.1
  441.1 1.6 reshape.199
  442.7 2.2 convolution_bitcast_fusion.1
  444.9 13.7 %fusion.23 = f32[2,16,32,32]{3,0,2,1:T(2,128)S(1)} fusion(f32[32,32]{1,0:T(8,128)S(1)} %fusion.43, f32[16,32]{1,0:T(8,128)S(1)} %get-tuple-element.35, pred[32,32]{1,0:T(8,128)(4,1)S(1)} %fusion.44, f32[2,16,32,32]{3,1,0,2:T(8,128)S(1)} %convolution_bitcast_fusion.1, f32[16,32,32]{2,1,0:T(8,128)S(1)} %exponential_multiply_fusion), kind=kOutput, calls=%fused_computation.28 | convolution fusion | flops 13664256 | bytes 334848 | tf_op jit(solution)/shard_map/while/body/eval_jaxpr/mgnk,bmgk->bmgn/dot_general | solution.py:37
  458.6 8.7 fusion
  467.3 3.8 add_bitcast_fusion
  471.1 7.8 copy.154
  479.0 7.8 copy.132
  486.8 0.0 all-to-all-done
  486.8 3.5 convert_bitcast_fusion
  490.2 11.7 %copy.122 = f32[2,32,64,128]{1,0,3,2:T(2,128)} copy(f32[2,32,64,128]{3,0,1,2:T(2,128)} %convert_bitcast_fusion) | data formatting | bytes 4194304 | tf_op jit(solution)/shard_map/convert_element_type | solution.py:97
  502.0 11.1 %fusion.4 = bf16[2,32,8192]{1,0,2:T(2,128)(2,1)} fusion(f32[2,32,64,128]{1,0,3,2:T(2,128)} %copy.132, f32[2,32,32,256]{1,0,3,2:T(2,128)} %copy.154, f32[2,32,64,128]{1,0,3,2:T(2,128)} %copy.122, f32[32]{0:T(128)S(1)} %dynamic_slice.25), kind=kLoop, calls=%fused_computation.6 | loop fusion | flops 2097152 | bytes 7340160 | tf_op jit(solution)/shard_map/convert_element_type | solution.py:97
  513.1 10.1 %reshape.228 = bf16[64,2,4096]{2,1,0:T(2,128)(2,1)} reshape(bf16[8192,2,32]{2,1,0:T(2,128)(2,1)} %bitcast.141) | data formatting | bytes 2097152
  523.1 10.6 %all-to-all-start.2 = ((bf16[64,2,4096]{2,1,0:T(2,128)(2,1)}), bf16[64,2,4096]{2,1,0:T(2,128)(2,1)S(1)}, u32[]{:S(2)}, u32[]{:S(2)}) async-start(bf16[64,2,4096]{2,1,0:T(2,128)(2,1)} %reshape.228), calls=%async_computation.2 | async-start | bytes 2097152 | tf_op jit(solution)/shard_map/all_to_all | solution.py:98
  533.7 0.0 reduce-scatter.7.cloned.1.call-start
  533.8 0.0 copy-done
  533.8 0.0 copy-done.3
  533.8 0.4 convolution_bitcast_fusion
  534.2 3.0 copy.155
  537.2 5.2 reshape.224
  542.4 0.0 reduce-scatter.7.cloned.1.call-update
  542.5 0.0 reduce-scatter.9.cloned.1.call-start
  542.5 287.7 %reduce-scatter.7.cloned.1.call-done = f32[32,24]{1,0:T(8,128)} async-done(((f32[2048,24]{1,0:T(8,128)}), f32[32,24]{1,0:T(8,128)}) %reduce-scatter.7.cloned.1.call-update) | async-done | bytes 3088
  830.2 0.8 reshape.225
  831.0 0.1 copy.156
  831.2 1.6 slice.73
  832.8 2.0 slice.74
  834.9 0.3 copy.136
  835.1 1.4 copy.137
  836.6 0.1 copy.149
  836.7 90.6 %all_gather.3 = bf16[2,4,2048]{1,0,2:T(2,128)(2,1)} all-gather(bf16[2,4,32]{1,0,2:T(2,128)(2,1)S(1)} %copy.149), channel_id=1, replica_groups=mesh['seq'=64,'chan'=4] {'seq'}, dimensions={2}, use_global_device_ids=true | all-gather | bytes 33280 | tf_op jit(solution)/shard_map/all_gather | solution.py:131
  927.3 2.6 copy.150
  929.9 2.0 convolution_bitcast_fusion.2
  931.9 0.0 reduce-scatter.9.cloned.1.call-update
  931.9 22.0 %reduce-scatter.9.cloned.1.call-done = f32[32,8]{1,0:T(8,128)} async-done(((f32[128,8]{1,0:T(8,128)}), f32[32,8]{1,0:T(8,128)}) %reduce-scatter.9.cloned.1.call-update) | async-done | bytes 1040
  953.9 1.4 copy.158
  955.3 0.0 all-to-all-done.2
  955.3 3.5 reshape.229
  958.8 9.0 copy.134
  (27 shorter events, 0.3 us)
Async XLA Ops:
  7.2 526.6 %copy-start = (bf16[3,128,2048]{2,1,0:T(8,128)(2,1)S(1)}, bf16[3,128,2048]{2,1,0:T(8,128)(2,1)}, u32[]{:S(2)}) copy-start(bf16[3,128,2048]{2,1,0:T(8,128)(2,1)} %param.18) | copy-start | bytes 4718596
  7.2 27.9 %copy-start.5 = (s32[2,4]{1,0:T(2,128)S(1)}, s32[2,4]{1,0:T(2,128)}, u32[]{:S(2)}) copy-start(s32[2,4]{1,0:T(2,128)} %param.12) | copy-start | bytes 100
  7.2 28.1 %copy-start.4 = (bf16[512,128]{1,0:T(8,128)(2,1)S(1)}, bf16[512,128]{1,0:T(8,128)(2,1)}, u32[]{:S(2)}) copy-start(bf16[512,128]{1,0:T(8,128)(2,1)} %param.16) | copy-start | bytes 393220
  24.7 26.0 %all-to-all-start.1 = ((bf16[2,2048,128]{2,0,1:T(2,128)(2,1)}), bf16[2,2048,128]{2,0,1:T(2,128)(2,1)S(1)}, u32[]{:S(2)}, u32[]{:S(2)}) async-start(bf16[2,2048,128]{2,0,1:T(2,128)(2,1)} %fusion.19), calls=%async_computation.1 | async-start | bytes 2097152 | tf_op jit(solution)/shard_map/all_to_all | solution.py:91
  50.6 436.1 %all-to-all-start = ((bf16[2,2048,128]{2,0,1:T(2,128)(2,1)}), bf16[2,2048,128]{2,0,1:T(2,128)(2,1)}, u32[]{:S(2)}, u32[]{:S(2)}) async-start(bf16[2,2048,128]{2,0,1:T(2,128)(2,1)} %bitcast.137), calls=%async_computation | async-start | bytes 2097152 | tf_op jit(solution)/shard_map/all_to_all | solution.py:90
  444.9 13.7 %copy-start.1 = (f32[2,16,32,32]{3,1,0,2:T(8,128)}, f32[2,16,32,32]{3,1,0,2:T(8,128)S(1)}, u32[]{:S(2)}) copy-start(f32[2,16,32,32]{3,1,0,2:T(8,128)S(1)} %convolution_bitcast_fusion.1) | copy-start | bytes 393220
  458.6 8.7 copy-start.2
  502.0 31.9 %copy-start.3 = (f32[128]{0:T(128)S(1)}, f32[128]{0:T(128)}, u32[]{:S(2)}) copy-start(f32[128]{0:T(128)} %param.17) | copy-start | bytes 1540
  523.1 432.1 %all-to-all-start.2 = ((bf16[64,2,4096]{2,1,0:T(2,128)(2,1)}), bf16[64,2,4096]{2,1,0:T(2,128)(2,1)S(1)}, u32[]{:S(2)}, u32[]{:S(2)}) async-start(bf16[64,2,4096]{2,1,0:T(2,128)(2,1)} %reshape.228), calls=%async_computation.2 | async-start | bytes 2097152 | tf_op jit(solution)/shard_map/all_to_all | solution.py:98
  533.7 296.5 %reduce-scatter.7.cloned.1.call-start = ((), (), s32[]{:S(2)}) async-start(), calls=%async_computation.5 | async-start | bytes 1064960
  542.5 411.5 %reduce-scatter.9.cloned.1.call-start = ((), (), s32[]{:S(2)}) async-start(), calls=%async_computation.6 | async-start | bytes 81920
Sparse Core Ops, SparseCore 0:
  542.6 287.5 reduce-scatter.6
  932.0 21.8 reduce-scatter.8
where the time goes:
time: 986 us; the launch traced here: 975 us
  waiting for transfers between devices  321 us (33%)
  local copies, waits for them, and re-layouts  318 us (32%)
  blocking collectives  232 us (24%)
  other arithmetic  33 us (3%)
  matrix products  31.1 us (3%)
  starting transfers between devices  25.8 us (3%)
  between operations  14.8 us (2%)
    unnamed x4, waiting for transfers between devices  310 us
    gather x2, local copies, waits for them, and re-layouts, one_group(): jnp.take(filt, jnp.maximum(distance, 0), axis=1)  239 us
    psum x1, blocking collectives, body(): total_sq = lax.psum(partial_sq, 'seq')  142 us
    all_gather x1, blocking collectives, body(): piece = lax.all_gather(decode_mix, 'seq', axis=2, tiled=True)  90.6 us
    unnamed x21, local copies, waits for them, and re-layouts  27.9 us
  transfers between devices with their start and end apart: 5, of which 3 were waited for; matrix products, arithmetic and copies ran while one was open for 32% of the time, Pallas kernels for 0%

commit v1 on v0

--- a/solution.py
+++ b/solution.py
@@ -128,7 +128,9 @@
         conv_step = jnp.sum(own_residue[None] * running, axis=1) + own_skip[None] * mixed_in
         outputs.append((projected[0, :, step].astype(jnp.float32) * conv_step).astype(jnp.bfloat16))
     decode_mix = jnp.stack(outputs, axis=1)
-    piece = lax.all_gather(decode_mix, "seq", axis=2, tiled=True)
+    piece = jnp.concatenate(
+        lax.all_to_all(jnp.stack([decode_mix] * lax.axis_size("seq")), "seq", 0, 0), axis=2
+    )
     piece_width = piece.shape[2]
     summed = jnp.dot(piece.reshape(-1, piece_width), out_weight, preferred_element_type=jnp.float32)
     decoded = lax.psum_scatter(summed, "chan", scatter_dimension=1, tiled=True).astype(jnp.bfloat16)

time: 986 us -> 650 us (0.66)
  waiting for transfers between devices: 321 us -> 65.2 us
  blocking collectives: 232 us -> 141 us
  starting transfers between devices: 25.8 us -> 37.9 us
    unnamed x4, waiting for transfers between devices: 310 us -> 65.2 us
    all_gather x1 -> x0, blocking collectives: 90.6 us -> none  [body(): piece = lax.all_gather(decode_mix, 'seq', axis=2, tiled=True)]
    all_to_all x1, waiting for transfers between devices: 10.8 us -> 0.01 us  [body(): lax.all_to_all(product, 'seq', split_axis=1, concat_axis=2, tiled=True)]
    unnamed x21 -> x31, local copies, waits for them, and re-layouts: 27.9 us -> 36.3 us
  transfers between devices with their start and end apart: 5 -> 6, of which waited for: 3 -> 2; matrix products, arithmetic and copies ran while one was open for 32% -> 55% of each run, Pallas kernels for 0% -> 0%
where the time goes in v1:
time: 650 us; the launch traced here: 642 us
  local copies, waits for them, and re-layouts  320 us (49%)
  blocking collectives  141 us (22%)
  waiting for transfers between devices  65.2 us (10%)
  starting transfers between devices  37.9 us (6%)
  other arithmetic  33 us (5%)
  matrix products  30 us (5%)
  between operations  14.5 us (2%)
    gather x2, local copies, waits for them, and re-layouts, one_group(): jnp.take(filt, jnp.maximum(distance, 0), axis=1)  239 us
    psum x1, blocking collectives, body(): total_sq = lax.psum(partial_sq, 'seq')  141 us
    unnamed x4, waiting for transfers between devices  65.2 us
    unnamed x31, local copies, waits for them, and re-layouts  36.3 us
    dot_general x1, matrix products, one_group(): jnp.einsum('mgnk,bmgk->bmgn', spread, block_sums, precision=highest)  13.9 us
    convert_element_type x2, other arithmetic, body(): gated = (query_part.astype(jnp.float32) * conv).astype(jnp.bfloat16)  13.4 us
    convert_element_type x1, other arithmetic, body(): product = jnp.where(live[:, None, :], keys_in.astype(jnp.float32) * value...  13.2 us
  transfers between devices with their start and end apart: 6, of which 2 were waited for; matrix products, arithmetic and copies ran while one was open for 55% of the time, Pallas kernels for 0%

profile of v1, /device:TPU:2, one launch (start us, length us, event | category | flops | bytes accessed | tf_op | source)
XLA Modules:
  0.0 642.1 jit_solution(967754967729831648)
XLA Ops:
  7.2 0.0 copy-start
  7.2 3.5 fusion.69
  10.7 0.7 broadcast_compare_fusion
  11.4 13.2 %fusion.19 = bf16[2,2048,128]{2,0,1:T(2,128)(2,1)} fusion(pred[2,128]{1,0:T(4,128)(4,1)S(1)} %broadcast_compare_fusion, bf16[1,2,2048,128]{3,2,1,0:T(8,128)(2,1)} %get-tuple-element.31, bf16[1,2,2048,128]{3,2,1,0:T(8,128)(2,1)S(1)} %get-tuple-element.30), kind=kLoop, calls=%fused_computation.24 | loop fusion | flops 2621440 | bytes 3145984 | tf_op jit(solution)/shard_map/convert_element_type | solution.py:85
  24.6 9.4 %all-to-all-start.1 = ((bf16[2,2048,128]{2,0,1:T(2,128)(2,1)}), bf16[2,2048,128]{2,0,1:T(2,128)(2,1)S(1)}, u32[]{:S(2)}, u32[]{:S(2)}) async-start(bf16[2,2048,128]{2,0,1:T(2,128)(2,1)} %fusion.19), calls=%async_computation.1 | async-start | bytes 2097152 | tf_op jit(solution)/shard_map/all_to_all | solution.py:91
  34.0 0.0 reduce-scatter.7.cloned.1.call-start
  34.1 0.1 eq.15
  34.2 0.3 multiply_reduce_fusion.5
  34.5 141.4 %psum.7 = f32[8]{0:T(128)S(1)} all-reduce(f32[8]{0:T(128)S(1)} %get-tuple-element.52), channel_id=1, replica_groups=mesh['seq'=64,'chan'=4] {'seq'}, use_global_device_ids=true, to_apply=%region_2.3 | all-reduce | flops 8 | bytes 64 | tf_op jit(solution)/shard_map/psum | solution.py:107
  175.9 0.4 convolution_bitcast_fusion
  176.2 3.1 copy.156
  179.3 5.3 reshape.226
  184.5 0.0 reduce-scatter.7.cloned.1.call-update
  184.6 0.1 copy.175
  184.8 0.8 fusion.68
  185.6 0.1 copy.128
  185.7 0.1 copy.127
  185.8 0.3 multiply_reduce_fusion
  186.0 0.1 fusion.44
  186.1 0.1 fusion.43
  186.2 0.8 dynamic_slice.25
  186.9 0.1 copy.129
  187.0 217.0 %gather_fusion = f32[65536,32]{1,0:T(8,128)} fusion(f32[32,256]{0,1:T(8,128)S(1)} %copy.129, s32[65536]{0:T(1024)S(1)} %broadcast_clamp_fusion), kind=kCustom, calls=%fused_computation | custom fusion | bytes 17039360 | tf_op jit(solution)/shard_map/while/body/eval_jaxpr/jit(_take)/gather | solution.py:25
  404.1 22.4 %copy.130 = f32[256,256,32]{1,0,2:T(8,128)} copy(f32[256,256,32]{2,1,0:T(8,128)} %bitcast.141) | data formatting | bytes 16777216 | tf_op jit(solution)/shard_map/while/body/eval_jaxpr/jit(_take)/gather | solution.py:25
  426.4 9.4 %copy.214 = bf16[1,2,2048,128]{3,1,2,0:T(2,128)(2,1)} copy(bf16[1,2,2048,128]{3,2,1,0:T(8,128)(2,1)S(1)} %copy-done.3) | data formatting | bytes 2097152
  435.9 0.1 maximum_compare_fusion
  436.0 0.1 exponential_multiply_fusion
  436.1 37.3 %reduce-scatter.7.cloned.1.call-done = f32[32,24]{1,0:T(8,128)} async-done(((f32[2048,24]{1,0:T(8,128)}), f32[32,24]{1,0:T(8,128)}) %reduce-scatter.7.cloned.1.call-update) | async-done | bytes 3088
  473.4 0.8 reshape.227
  474.2 0.1 copy.157
  474.4 0.0 all-to-all-done.1
  474.4 0.0 copy-start.2
  474.4 1.0 copy-done.2
  475.4 10.6 %all-to-all-start = ((bf16[2,2048,128]{2,0,1:T(2,128)(2,1)}), bf16[2,2048,128]{2,0,1:T(2,128)(2,1)S(1)}, u32[]{:S(2)}, u32[]{:S(2)}) async-start(bf16[2,2048,128]{2,0,1:T(2,128)(2,1)} %bitcast.140), calls=%async_computation | async-start | bytes 2097152 | tf_op jit(solution)/shard_map/all_to_all | solution.py:90
  486.0 4.1 copy_bitcast_fusion.1
  490.1 1.6 reshape.201
  491.7 2.2 convolution_bitcast_fusion.1
  493.9 0.2 slice.74
  494.1 13.9 %fusion.23 = f32[2,16,32,32]{3,0,2,1:T(2,128)S(1)} fusion(f32[32,32]{1,0:T(8,128)S(1)} %fusion.43, f32[16,32]{1,0:T(8,128)S(1)} %get-tuple-element.35, pred[32,32]{1,0:T(8,128)(4,1)S(1)} %fusion.44, f32[2,16,32,32]{3,1,0,2:T(8,128)S(1)} %convolution_bitcast_fusion.1, f32[16,32,32]{2,1,0:T(8,128)S(1)} %exponential_multiply_fusion), kind=kOutput, calls=%fused_computation.28 | convolution fusion | flops 13664256 | bytes 334848 | tf_op jit(solution)/shard_map/while/body/eval_jaxpr/mgnk,bmgk->bmgn/dot_general | solution.py:37
  508.0 0.8 copy-done.4
  508.8 0.6 slice.73
  509.4 0.3 copy.137
  509.6 0.4 copy.138
  510.1 0.7 reshape.232
  510.9 8.5 %fusion = f32[32,2,32,256]{3,2,1,0:T(8,128)S(1)} fusion(bf16[2,32,32,256]{3,2,0,1:T(8,128)(2,1)S(1)} %reshape.201, f32[256,256,32]{1,0,2:T(8,128)} %copy.130, pred[256,256]{1,0:T(8,128)(4,1)S(1)} %get-tuple-element.56, pred[256,256]{1,0:T(8,128)(4,1)S(1)} %get-tuple-element.55), kind=kOutput, calls=%fused_computation.1 | convolution fusion | flops 1614807040 | bytes 11665408 | tf_op jit(solution)/shard_map/while/body/eval_jaxpr/gij,bgnj->bgni/dot_general | solution.py:27
  519.4 3.8 add_bitcast_fusion
  523.2 7.8 %copy.155 = f32[2,32,32,256]{1,0,3,2:T(2,128)} copy(f32[2,32,32,256]{3,2,0,1:T(8,128)} %add_bitcast_fusion) | data formatting | bytes 4194304 | tf_op jit(solution)/shard_map/while/body/eval_jaxpr/reshape | solution.py:43
  531.0 7.8 %copy.133 = f32[2,32,64,128]{1,0,3,2:T(2,128)} copy(f32[2,32,64,128]{3,2,0,1:T(8,128)} %get-tuple-element.33) | data formatting | bytes 4194304 | tf_op jit(solution)/shard_map/convert_element_type | solution.py:95
  538.9 9.0 %all-to-all-start.3 = ((bf16[64,2,128]{2,1,0:T(2,128)(2,1)}), bf16[64,2,128]{2,1,0:T(2,128)(2,1)S(1)}, u32[]{:S(2)}, u32[]{:S(2)}) async-start(bf16[64,2,128]{2,1,0:T(2,128)(2,1)} %reshape.232), calls=%async_computation.3 | async-start | bytes 65536 | tf_op jit(solution)/shard_map/all_to_all | solution.py:132
  547.9 2.2 convert_bitcast_fusion
  550.1 11.8 %copy.123 = f32[2,32,64,128]{1,0,3,2:T(2,128)} copy(f32[2,32,64,128]{3,0,1,2:T(2,128)} %convert_bitcast_fusion) | data formatting | bytes 4194304 | tf_op jit(solution)/shard_map/convert_element_type | solution.py:97
  561.9 11.2 %fusion.4 = bf16[2,32,8192]{1,0,2:T(2,128)(2,1)} fusion(f32[2,32,64,128]{1,0,3,2:T(2,128)} %copy.133, f32[2,32,32,256]{1,0,3,2:T(2,128)} %copy.155, f32[2,32,64,128]{1,0,3,2:T(2,128)} %copy.123, f32[32]{0:T(128)S(1)} %dynamic_slice.25), kind=kLoop, calls=%fused_computation.6 | loop fusion | flops 2097152 | bytes 7340160 | tf_op jit(solution)/shard_map/convert_element_type | solution.py:97
  573.0 10.0 %reshape.230 = bf16[64,2,4096]{2,1,0:T(2,128)(2,1)} reshape(bf16[8192,2,32]{2,1,0:T(2,128)(2,1)} %bitcast.144) | data formatting | bytes 2097152
  583.0 8.9 %all-to-all-start.2 = ((bf16[64,2,4096]{2,1,0:T(2,128)(2,1)}), bf16[64,2,4096]{2,1,0:T(2,128)(2,1)S(1)}, u32[]{:S(2)}, u32[]{:S(2)}) async-start(bf16[64,2,4096]{2,1,0:T(2,128)(2,1)} %reshape.230), calls=%async_computation.2 | async-start | bytes 2097152 | tf_op jit(solution)/shard_map/all_to_all | solution.py:98
  591.9 0.0 reduce-scatter.9.cloned.1.call-start
  592.0 0.1 reshape.233
  592.1 0.2 reshape_reshape.3
  592.3 1.0 convolution_bitcast_fusion.2
  593.3 0.0 reduce-scatter.9.cloned.1.call-update
  593.3 27.8 %reduce-scatter.9.cloned.1.call-done = f32[32,8]{1,0:T(8,128)} async-done(((f32[128,8]{1,0:T(8,128)}), f32[32,8]{1,0:T(8,128)}) %reduce-scatter.9.cloned.1.call-update) | async-done | bytes 1040
  621.1 1.4 copy.159
  622.5 0.0 all-to-all-done.2
  622.5 3.5 reshape.231
  626.0 9.0 %copy.135 = bf16[2,64,32,128]{3,2,1,0:T(8,128)(2,1)} copy(bf16[2,64,32,128]{2,0,3,1:T(2,128)(2,1)} %bitcast.142) | data formatting | bytes 2097152 | tf_op jit(solution)/shard_map/all_to_all | solution.py:98
  (39 shorter events, 0.3 us)
Async XLA Ops:
  7.2 168.7 %copy-start = (bf16[3,128,2048]{2,1,0:T(8,128)(2,1)S(1)}, bf16[3,128,2048]{2,1,0:T(8,128)(2,1)}, u32[]{:S(2)}) copy-start(bf16[3,128,2048]{2,1,0:T(8,128)(2,1)} %param.18) | copy-start | bytes 4718596
  7.2 26.9 %copy-start.9 = (s32[2,4]{1,0:T(2,128)S(1)}, s32[2,4]{1,0:T(2,128)}, u32[]{:S(2)}) copy-start(s32[2,4]{1,0:T(2,128)} %param.12) | copy-start | bytes 100
  7.2 27.0 %copy-start.8 = (bf16[512,128]{1,0:T(8,128)(2,1)S(1)}, bf16[512,128]{1,0:T(8,128)(2,1)}, u32[]{:S(2)}) copy-start(bf16[512,128]{1,0:T(8,128)(2,1)} %param.16) | copy-start | bytes 393220
  7.2 168.7 %copy-start.7 = (f32[128]{0:T(128)S(1)}, f32[128]{0:T(128)}, u32[]{:S(2)}) copy-start(f32[128]{0:T(128)} %param.17) | copy-start | bytes 1540
  24.6 449.8 %all-to-all-start.1 = ((bf16[2,2048,128]{2,0,1:T(2,128)(2,1)}), bf16[2,2048,128]{2,0,1:T(2,128)(2,1)S(1)}, u32[]{:S(2)}, u32[]{:S(2)}) async-start(bf16[2,2048,128]{2,0,1:T(2,128)(2,1)} %fusion.19), calls=%async_computation.1 | async-start | bytes 2097152 | tf_op jit(solution)/shard_map/all_to_all | solution.py:91
  34.0 439.4 %reduce-scatter.7.cloned.1.call-start = ((), (), s32[]{:S(2)}) async-start(), calls=%async_computation.6 | async-start | bytes 1064960
  404.1 22.4 %copy-start.3 = (bf16[1,2,2048,128]{3,2,1,0:T(8,128)(2,1)S(1)}, bf16[1,2,2048,128]{3,2,1,0:T(8,128)(2,1)}, u32[]{:S(2)}) copy-start(bf16[1,2,2048,128]{3,2,1,0:T(8,128)(2,1)} %get-tuple-element.29) | copy-start | bytes 3145732
  474.4 1.0 copy-start.2
  475.4 63.5 %all-to-all-start = ((bf16[2,2048,128]{2,0,1:T(2,128)(2,1)}), bf16[2,2048,128]{2,0,1:T(2,128)(2,1)S(1)}, u32[]{:S(2)}, u32[]{:S(2)}) async-start(bf16[2,2048,128]{2,0,1:T(2,128)(2,1)} %bitcast.140), calls=%async_computation | async-start | bytes 2097152 | tf_op jit(solution)/shard_map/all_to_all | solution.py:90
  508.0 0.8 copy-start.4
  509.6 9.8 %copy-start.5 = (f32[2,16,32,32]{3,0,2,1:T(2,128)S(1)}, f32[2,16,32,32]{3,0,2,1:T(2,128)}, u32[]{:S(2)}) copy-start(f32[2,16,32,32]{3,0,2,1:T(2,128)} %copy-done.4) | copy-start | bytes 393220
  538.9 44.1 %all-to-all-start.3 = ((bf16[64,2,128]{2,1,0:T(2,128)(2,1)}), bf16[64,2,128]{2,1,0:T(2,128)(2,1)S(1)}, u32[]{:S(2)}, u32[]{:S(2)}) async-start(bf16[64,2,128]{2,1,0:T(2,128)(2,1)} %reshape.232), calls=%async_computation.3 | async-start | bytes 65536 | tf_op jit(solution)/shard_map/all_to_all | solution.py:132
  561.9 30.4 %copy-start.6 = (bf16[2048,128]{1,0:T(8,128)(2,1)S(1)}, bf16[2048,128]{1,0:T(8,128)(2,1)}, u32[]{:S(2)}) copy-start(bf16[2048,128]{1,0:T(8,128)(2,1)} %param.19) | copy-start | bytes 1572868
  573.0 62.0 %copy-start.1 = (bf16[3,128,2048]{2,1,0:T(8,128)(2,1)S(1)}, bf16[3,128,2048]{2,1,0:T(8,128)(2,1)}, u32[]{:S(2)}) copy-start(bf16[3,128,2048]{2,1,0:T(8,128)(2,1)} %param.18) | copy-start | bytes 4718596
  583.0 39.5 %all-to-all-start.2 = ((bf16[64,2,4096]{2,1,0:T(2,128)(2,1)}), bf16[64,2,4096]{2,1,0:T(2,128)(2,1)S(1)}, u32[]{:S(2)}, u32[]{:S(2)}) async-start(bf16[64,2,4096]{2,1,0:T(2,128)(2,1)} %reshape.230), calls=%async_computation.2 | async-start | bytes 2097152 | tf_op jit(solution)/shard_map/all_to_all | solution.py:98
  591.9 29.2 %reduce-scatter.9.cloned.1.call-start = ((), (), s32[]{:S(2)}) async-start(), calls=%async_computation.7 | async-start | bytes 81920
Sparse Core Ops, SparseCore 0:
  184.7 288.6 reduce-scatter.6
  595.2 25.8 reduce-scatter.8
